TPU v7x, 32 devices: a whole 2x2x4 slice. The times are simulated.
32 devices in a mesh: dp: 4 (over y, core), seq: 8 (over z, x).
Axes of the slice: x: 2, y: 2, z: 4, core: 2. Of those that a mesh axis runs over, the one named last changes fastest.
Arguments:
- query: bfloat16 [8, 2048, 32, 128], P('dp', 'seq'), may hold values from -128 to 128
- keys: bfloat16 [8, 2048, 4, 128], P('dp', 'seq'), may hold values from -4.5 to 4.5
- values: bfloat16 [8, 2048, 4, 128], P('dp', 'seq'), may hold values from -6 to 6
- output: bfloat16 [8, 2048, 32, 128], P('dp', 'seq'), may hold values from -6 to 6
- out_grad: bfloat16 [8, 2048, 32, 128], P('dp', 'seq'), may hold values from -6 to 6
- lengths: int32 [8], P('dp'), may hold values from 341 to 2048, as said below
- margins: float32 [4], P('dp'), may hold values from -3 to 3
Outputs:
- query_grad: bfloat16 [8, 2048, 32, 128], P('dp', 'seq')
- key_grad: bfloat16 [8, 2048, 4, 128], P('dp', 'seq')
- value_grad: bfloat16 [8, 2048, 4, 128], P('dp', 'seq')
Inputs may be any that keep to these rules, and one draw needn't show every extreme that they name: `lengths`: sequence 2p is pair p's chosen response and 2p + 1 its rejected one; some sequence has exactly 2048 tokens.
All inputs are finite; a program needn't handle non-finite values.
Results may differ from a plain program's by a relative error of at most 0.009.
Values may be sent and summed in bfloat16 or wider, within the bound.
A program may use at most 128 MiB of HBM per device.

v0:
```python
import math
import jax
import jax.numpy as jnp
from jax import lax
from jax.sharding import PartitionSpec as P


def sequence_grads(query, scaled, keys, values, delta, length):
    full_len, per_dev, head_dim = query.shape
    slots = keys.shape[1]
    repeat = per_dev // slots
    block = min(512, full_len)
    scale = 1.0 / math.sqrt(head_dim)
    q_four = query.reshape(full_len, slots, repeat, head_dim)
    g_four = scaled.reshape(full_len, slots, repeat, head_dim)
    d_three = delta.reshape(full_len, slots, repeat)

    def make_step(start):
        prefix = start + block

        def one_block(carry):
            query_all, key_acc, value_acc = carry
            q_block = q_four[start:prefix]
            g_block = g_four[start:prefix]
            d_block = jnp.transpose(d_three[start:prefix], (1, 2, 0))[..., None]
            key_pre = keys[:prefix]
            value_pre = values[:prefix]
            scores = (
                jnp.einsum("isrd,jsd->srij", q_block, key_pre, preferred_element_type=jnp.float32)
                * scale
            )
            query_pos = start + jnp.arange(block)
            causal = jnp.arange(prefix)[None, :] <= query_pos[:, None]
            scores = jnp.where(causal, scores, -jnp.inf)
            top = jnp.max(scores, axis=-1, keepdims=True)
            lse = top + jnp.log(jnp.sum(jnp.exp(scores - top), axis=-1, keepdims=True))
            prob = jnp.exp(scores - lse)
            prob_low = prob.astype(jnp.bfloat16)
            value_part = jnp.einsum(
                "srij,isrd->jsd", prob_low, g_block, preferred_element_type=jnp.float32
            )
            dprob = jnp.einsum(
                "isrd,jsd->srij", g_block, value_pre, preferred_element_type=jnp.float32
            )
            dscore = prob * (dprob - d_block)
            dscore_low = dscore.astype(jnp.bfloat16)
            query_part = (
                jnp.einsum(
                    "srij,jsd->isrd", dscore_low, key_pre, preferred_element_type=jnp.float32
                )
                * scale
            )
            query_part = query_part.reshape(block, per_dev, head_dim).astype(jnp.bfloat16)
            query_all = lax.dynamic_update_slice_in_dim(query_all, query_part, start, 0)
            key_part = jnp.einsum(
                "srij,isrd->jsd", dscore_low, q_block, preferred_element_type=jnp.float32
            )
            key_acc = key_acc.at[:prefix].add(key_part)
            value_acc = value_acc.at[:prefix].add(value_part)
            return (query_all, key_acc, value_acc)

        return one_block

    carry = (
        jnp.zeros((full_len, per_dev, head_dim), jnp.bfloat16),
        jnp.zeros((full_len, slots, head_dim), jnp.float32),
        jnp.zeros((full_len, slots, head_dim), jnp.float32),
    )
    for index in range(full_len // block):
        start = index * block
        step_fn = make_step(start)
        carry = step_fn(carry)
    query_all, key_acc, value_acc = carry
    return (query_all, key_acc * scale, value_acc)


def body(query, keys, values, output, out_grad, lengths, margins):
    seq_size = lax.axis_size("seq")
    place = lax.axis_index("seq")
    seqs_dev, toks_dev, heads, head_dim = query.shape
    kv_heads = keys.shape[2]
    per_dev = heads // seq_size
    group = heads // kv_heads
    total = lax.psum(jnp.sum(lengths), "dp")
    mean_len = total.astype(jnp.float32) / (seqs_dev * lax.axis_size("dp"))
    weight = jax.nn.sigmoid(-margins)
    signs = jnp.tile(jnp.array([-1.0, 1.0], jnp.float32), margins.shape[0])
    coef = jnp.repeat(weight, 2) * signs * 4.0 * mean_len / lengths.astype(jnp.float32)
    positions = place * toks_dev + jnp.arange(toks_dev)
    live = (positions[None, :] < lengths[:, None]).astype(jnp.float32)
    factor = coef[:, None] * live
    scaled = (out_grad.astype(jnp.float32) * factor[:, :, None, None]).astype(jnp.bfloat16)
    copies = max(1, group // per_dev)
    key_slots = jnp.repeat(keys, copies, axis=2)
    value_slots = jnp.repeat(values, copies, axis=2)
    q_heads, g_heads, o_heads, k_heads, v_heads = (
        lax.all_to_all(query, "seq", split_axis=2, concat_axis=1, tiled=True),
        lax.all_to_all(scaled, "seq", split_axis=2, concat_axis=1, tiled=True),
        lax.all_to_all(output, "seq", split_axis=2, concat_axis=1, tiled=True),
        lax.all_to_all(key_slots, "seq", split_axis=2, concat_axis=1, tiled=True),
        lax.all_to_all(value_slots, "seq", split_axis=2, concat_axis=1, tiled=True),
    )
    delta = jnp.sum(g_heads.astype(jnp.float32) * o_heads.astype(jnp.float32), axis=3)
    query_heads, key_heads, value_heads = lax.map(
        lambda items: sequence_grads(*items), (q_heads, g_heads, k_heads, v_heads, delta, lengths)
    )
    query_grad = lax.all_to_all(query_heads, "seq", split_axis=1, concat_axis=2, tiled=True)
    key_rows, value_rows = (
        lax.all_to_all(key_heads, "seq", split_axis=1, concat_axis=2, tiled=True),
        lax.all_to_all(value_heads, "seq", split_axis=1, concat_axis=2, tiled=True),
    )
    key_grad = jnp.sum(
        key_rows.reshape(seqs_dev, toks_dev, kv_heads, copies, head_dim), axis=3
    ).astype(jnp.bfloat16)
    value_grad = jnp.sum(
        value_rows.reshape(seqs_dev, toks_dev, kv_heads, copies, head_dim), axis=3
    ).astype(jnp.bfloat16)
    return (query_grad, key_grad, value_grad)


def solution(mesh):
    return jax.shard_map(
        body,
        mesh=mesh,
        in_specs=(
            P("dp", "seq", None, None),
            P("dp", "seq", None, None),
            P("dp", "seq", None, None),
            P("dp", "seq", None, None),
            P("dp", "seq", None, None),
            P("dp"),
            P("dp"),
        ),
        out_specs=(
            P("dp", "seq", None, None),
            P("dp", "seq", None, None),
            P("dp", "seq", None, None),
        ),
        check_vma=False,
    )
```

profile of v0, /device:TPU:0, one launch (start us, length us, event | category | flops | bytes accessed | tf_op | source)
XLA Modules:
  0.0 792.0 jit_solution(2441812579054759764)
XLA Ops:
  3.0 7.3 all-to-all-start
  10.4 25.7 %all-to-all-done = bf16[2,256,8,128]{3,1,0,2:T(8,128)(2,1)S(1)} async-done(((bf16[2,256,8,128]{3,1,0,2:T(8,128)(2,1)}), bf16[2,256,8,128]{3,1,0,2:T(8,128)(2,1)S(1)}, u32[]{:S(2)}, u32[]{:S(2)}) %all-to-all-start) | async-done | bytes 1048608 | tf_op jit(solution)/shard_map/all_to_all | solution.py:100
  41.5 5.6 psum.7
  48.5 5.9 multiply_convert_fusion
  54.4 12.4 %all-to-all-done.2 = bf16[2,256,8,128]{3,1,0,2:T(8,128)(2,1)S(1)} async-done(((bf16[2,256,8,128]{3,1,0,2:T(8,128)(2,1)}), bf16[2,256,8,128]{3,1,0,2:T(8,128)(2,1)S(1)}, u32[]{:S(2)}, u32[]{:S(2)}) %all-to-all-start.2) | async-done | bytes 1048608 | tf_op jit(solution)/shard_map/all_to_all | solution.py:101
  71.3 5.8 copy.192
  77.2 86.7 %all-to-all-done.3 = bf16[2,256,32,128]{3,1,0,2:T(8,128)(2,1)} async-done(((bf16[2,256,32,128]{3,1,0,2:T(8,128)(2,1)}), bf16[2,256,32,128]{3,1,0,2:T(8,128)(2,1)}, u32[]{:S(2)}, u32[]{:S(2)}) %all-to-all-start.3) | async-done | bytes 4194336 | tf_op jit(solution)/shard_map/all_to_all | solution.py:98
  168.5 5.8 copy.198
  174.3 86.7 %all-to-all-done.1 = bf16[2,256,32,128]{3,1,0,2:T(8,128)(2,1)} async-done(((bf16[2,256,32,128]{3,1,0,2:T(8,128)(2,1)}), bf16[2,256,32,128]{3,1,0,2:T(8,128)(2,1)}, u32[]{:S(2)}, u32[]{:S(2)}) %all-to-all-start.1) | async-done | bytes 4194336 | tf_op jit(solution)/shard_map/all_to_all | solution.py:97
  277.2 80.9 %all-to-all-done.4 = bf16[2,256,32,128]{3,1,0,2:T(8,128)(2,1)} async-done(((bf16[2,256,32,128]{3,1,0,2:T(8,128)(2,1)}), bf16[2,256,32,128]{3,1,0,2:T(8,128)(2,1)}, u32[]{:S(2)}, u32[]{:S(2)}) %all-to-all-start.4) | async-done | bytes 4194336 | tf_op jit(solution)/shard_map/all_to_all | solution.py:99
  358.1 5.7 fusion.155
  363.9 221.8 %while.27 = (s32[]{:T(128)}, bf16[2,2048,4,128]{3,2,0,1:T(4,128)(2,1)}, f32[2,2048,1,128]{3,2,0,1:T(1,128)}, f32[2,2048,1,128]{3,2,0,1:T(1,128)}, bf16[2,2048,1,...) while((s32[]{:T(128)}, ...), condition=%wide.region_12.13_spmd, body=%wide.region_3.12_spmd.sunk | while | flops 13606184960 | bytes 444718720 | solution.py:104
  399.4 6.2 fusion.222
  405.6 5.7 fusion.215
  429.1 11.9 %fusion.223 = f32[1,2048,1,128]{1,3,2,0:T(8,128)} fusion(f32[2048,1,128]{0,2,1:T(8,128)} %fusion.222, f32[2048,512,4]{1,0,2:T(8,128)} %copy-done, f32[4,512]{1,0:T(4,128)S(1)} %log_add_fusion.11, pred[512,2048]{0,1:T(8,128)(4,1)S(1)} %copy-done.3, bf16[2,2048,4,128]{3,1,2,0:T(8,128)(2,1)} %get-tuple-element.461, s32[]{:T(128)S(6)} %copy.272, ...), kind=kOutput, calls=%fused_computation.58.clone.1 | convolution fusion | flops 1090781184 | bytes 20455432 | tf_op jit(solution)/shard_map/while/body/eval_jaxpr/srij,isrd->jsd/dot_general | solution.py:39
  441.0 9.0 %fusion.218 = bf16[4,512,2048]{1,2,0:T(8,128)(2,1)S(1)} fusion(f32[2048,512,4]{1,0,2:T(8,128)} %copy-done, f32[4,512]{1,0:T(4,128)S(1)} %get-tuple-element.420, f32[4,512]{1,0:T(4,128)S(1)} %log_add_fusion.11, pred[512,2048]{0,1:T(8,128)(4,1)S(1)} %copy-done.3, bf16[2,2048,1,128]{3,1,2,0:T(8,128)(2,1)S(1)} %copy-done.15, s32[]{:T(128)S(6)} %copy.272, ...), kind=kOutput, calls=%fused_computation.16.clone.1 | convolution fusion | flops 1098907648 | bytes 27280896 | tf_op jit(solution)/shard_map/while/body/eval_jaxpr/isrd,jsd->srij/dot_general | solution.py:42
  507.6 6.0 fusion.222
  513.6 5.7 fusion.215
  537.2 11.9 %fusion.223 = f32[1,2048,1,128]{1,3,2,0:T(8,128)} fusion(f32[2048,1,128]{0,2,1:T(8,128)} %fusion.222, f32[2048,512,4]{1,0,2:T(8,128)} %copy-done, f32[4,512]{1,0:T(4,128)S(1)} %log_add_fusion.11, pred[512,2048]{0,1:T(8,128)(4,1)S(1)} %copy-done.3, bf16[2,2048,4,128]{3,1,2,0:T(8,128)(2,1)} %get-tuple-element.461, s32[]{:T(128)S(6)} %copy.272, ...), kind=kOutput, calls=%fused_computation.58.clone.1 | convolution fusion | flops 1090781184 | bytes 20455432 | tf_op jit(solution)/shard_map/while/body/eval_jaxpr/srij,isrd->jsd/dot_general | solution.py:39
  549.1 9.0 %fusion.218 = bf16[4,512,2048]{1,2,0:T(8,128)(2,1)S(1)} fusion(f32[2048,512,4]{1,0,2:T(8,128)} %copy-done, f32[4,512]{1,0:T(4,128)S(1)} %get-tuple-element.420, f32[4,512]{1,0:T(4,128)S(1)} %log_add_fusion.11, pred[512,2048]{0,1:T(8,128)(4,1)S(1)} %copy-done.3, bf16[2,2048,1,128]{3,1,2,0:T(8,128)(2,1)S(1)} %copy-done.15, s32[]{:T(128)S(6)} %copy.272, ...), kind=kOutput, calls=%fused_computation.16.clone.1 | convolution fusion | flops 1098907648 | bytes 27280896 | tf_op jit(solution)/shard_map/while/body/eval_jaxpr/isrd,jsd->srij/dot_general | solution.py:42
  585.8 52.4 %all_to_all.129 = f32[2,2048,1,128]{3,2,0,1:T(1,128)} all-to-all(f32[2,2048,1,128]{3,2,0,1:T(1,128)} %get-tuple-element.269), channel_id=1, replica_groups=mesh['dp'=4,'seq'=8] {'seq'}, dimensions={1} | all-to-all | bytes 4194304 | tf_op jit(solution)/shard_map/all_to_all | solution.py:110
  638.2 51.2 %all_to_all.130 = f32[2,2048,1,128]{3,2,0,1:T(1,128)S(1)} all-to-all(f32[2,2048,1,128]{3,2,0,1:T(1,128)S(1)} %copy-done.14), channel_id=1, replica_groups=mesh['dp'=4,'seq'=8] {'seq'}, dimensions={1} | all-to-all | bytes 4194304 | tf_op jit(solution)/shard_map/all_to_all | solution.py:109
  702.8 83.4 %all-to-all-done.5 = bf16[2,2048,4,128]{3,2,0,1:T(4,128)(2,1)} async-done(((bf16[2,2048,4,128]{3,2,0,1:T(4,128)(2,1)}), bf16[2,2048,4,128]{3,2,0,1:T(4,128)(2,1)}, u32[]{:S(2)}, u32[]{:S(2)}) %all-to-all-start.5) | async-done | bytes 4194336 | tf_op jit(solution)/shard_map/all_to_all | solution.py:107
  786.2 5.6 copy.203
  (174 shorter events, 196.4 us)
Async XLA Ops:
  0.6 9.7 %copy-start.16 = (bf16[2,256,4,128]{3,2,1,0:T(4,128)(2,1)S(1)}, bf16[2,256,4,128]{3,2,1,0:T(4,128)(2,1)}, u32[]{:S(2)}) copy-start(bf16[2,256,4,128]{3,2,1,0:T(4,128)(2,1)} %param.32) | copy-start | bytes 1572868
  1.8 39.0 %copy-start.17 = (s32[2]{0:T(128)S(1)}, s32[2]{0:T(128)}, u32[]{:S(2)}) copy-start(s32[2]{0:T(128)} %param.35) | copy-start | bytes 28
  1.8 46.6 %copy-start.18 = (f32[2]{0:T(128)S(1)}, f32[2]{0:T(128)}, u32[]{:S(2)}) copy-start(f32[2]{0:T(128)} %constant.334.clone) | copy-start | bytes 28
  3.0 33.0 %all-to-all-start = ((bf16[2,256,8,128]{3,1,0,2:T(8,128)(2,1)}), bf16[2,256,8,128]{3,1,0,2:T(8,128)(2,1)S(1)}, u32[]{:S(2)}, u32[]{:S(2)}) async-start(bf16[2,256,8,128]{3,1,0,2:T(8,128)(2,1)} %bitcast.103), calls=%async_computation | async-start | bytes 2097152 | tf_op jit(solution)/shard_map/all_to_all | solution.py:100
  37.2 29.5 %all-to-all-start.2 = ((bf16[2,256,8,128]{3,1,0,2:T(8,128)(2,1)}), bf16[2,256,8,128]{3,1,0,2:T(8,128)(2,1)S(1)}, u32[]{:S(2)}, u32[]{:S(2)}) async-start(bf16[2,256,8,128]{3,1,0,2:T(8,128)(2,1)} %bitcast.628), calls=%async_computation.2 | async-start | bytes 2097152 | tf_op jit(solution)/shard_map/all_to_all | solution.py:101
  66.8 10.4 %copy-start.11 = (bf16[2,256,8,128]{3,1,0,2:T(8,128)(2,1)}, bf16[2,256,8,128]{3,1,0,2:T(8,128)(2,1)S(1)}, u32[]{:S(2)}) copy-start(bf16[2,256,8,128]{3,1,0,2:T(8,128)(2,1)S(1)} %all-to-all-done.2) | copy-start | bytes 3145732
  66.8 97.1 %all-to-all-start.3 = ((bf16[2,256,32,128]{3,1,0,2:T(8,128)(2,1)}), bf16[2,256,32,128]{3,1,0,2:T(8,128)(2,1)}, u32[]{:S(2)}, u32[]{:S(2)}) async-start(bf16[2,256,32,128]{3,1,0,2:T(8,128)(2,1)} %multiply_convert_fusion), calls=%async_computation.3 | async-start | bytes 8388608 | tf_op jit(solution)/shard_map/all_to_all | solution.py:98
  163.9 97.1 %all-to-all-start.1 = ((bf16[2,256,32,128]{3,1,0,2:T(8,128)(2,1)}), bf16[2,256,32,128]{3,1,0,2:T(8,128)(2,1)}, u32[]{:S(2)}, u32[]{:S(2)}) async-start(bf16[2,256,32,128]{3,1,0,2:T(8,128)(2,1)} %copy.192), calls=%async_computation.1 | async-start | bytes 8388608 | tf_op jit(solution)/shard_map/all_to_all | solution.py:97
  261.0 97.1 %all-to-all-start.4 = ((bf16[2,256,32,128]{3,1,0,2:T(8,128)(2,1)}), bf16[2,256,32,128]{3,1,0,2:T(8,128)(2,1)}, u32[]{:S(2)}, u32[]{:S(2)}) async-start(bf16[2,256,32,128]{3,1,0,2:T(8,128)(2,1)} %copy.198), calls=%async_computation.4 | async-start | bytes 8388608 | tf_op jit(solution)/shard_map/all_to_all | solution.py:99
  364.3 30.1 %copy-start.6 = (bf16[2,2048,1,128]{3,1,2,0:T(8,128)(2,1)}, bf16[2,2048,1,128]{3,1,2,0:T(8,128)(2,1)S(1)}, u32[]{:S(2)}) copy-start(bf16[2,2048,1,128]{3,1,2,0:T(8,128)(2,1)S(1)} %get-tuple-element.458) | copy-start | bytes 3145732 | tf_op jit(solution)/shard_map/while
  365.4 34.0 %copy-start.9 = (pred[512,1536]{0,1:T(8,128)(4,1)}, pred[512,1536]{0,1:T(8,128)(4,1)S(1)}, u32[]{:S(2)}) copy-start(pred[512,1536]{0,1:T(8,128)(4,1)S(1)} %iota_compare_fusion.10) | copy-start | bytes 2359300 | tf_op jit(solution)/shard_map/while
  423.4 5.7 copy-start
  429.1 11.9 %copy-start.15 = (bf16[2,2048,1,128]{3,1,2,0:T(8,128)(2,1)S(1)}, bf16[2,2048,1,128]{3,1,2,0:T(8,128)(2,1)}, u32[]{:S(2)}) copy-start(bf16[2,2048,1,128]{3,1,2,0:T(8,128)(2,1)} %get-tuple-element.460) | copy-start | bytes 3145732 | tf_op jit(solution)/shard_map/while
  441.0 9.0 %copy-start.2 = (f32[2048,1,128]{0,2,1:T(8,128)S(1)}, f32[2048,1,128]{0,2,1:T(8,128)}, u32[]{:S(2)}) copy-start(f32[2048,1,128]{0,2,1:T(8,128)} %fusion.226) | copy-start | bytes 3145732 | tf_op jit(solution)/shard_map/while
  450.1 5.0 copy-start.7
  472.3 30.3 %copy-start.6 = (bf16[2,2048,1,128]{3,1,2,0:T(8,128)(2,1)}, bf16[2,2048,1,128]{3,1,2,0:T(8,128)(2,1)S(1)}, u32[]{:S(2)}) copy-start(bf16[2,2048,1,128]{3,1,2,0:T(8,128)(2,1)S(1)} %get-tuple-element.458) | copy-start | bytes 3145732 | tf_op jit(solution)/shard_map/while
  473.4 34.2 %copy-start.9 = (pred[512,1536]{0,1:T(8,128)(4,1)}, pred[512,1536]{0,1:T(8,128)(4,1)S(1)}, u32[]{:S(2)}) copy-start(pred[512,1536]{0,1:T(8,128)(4,1)S(1)} %iota_compare_fusion.10) | copy-start | bytes 2359300 | tf_op jit(solution)/shard_map/while
  531.4 5.7 copy-start
  537.1 11.9 %copy-start.15 = (bf16[2,2048,1,128]{3,1,2,0:T(8,128)(2,1)S(1)}, bf16[2,2048,1,128]{3,1,2,0:T(8,128)(2,1)}, u32[]{:S(2)}) copy-start(bf16[2,2048,1,128]{3,1,2,0:T(8,128)(2,1)} %get-tuple-element.460) | copy-start | bytes 3145732 | tf_op jit(solution)/shard_map/while
  549.1 9.0 %copy-start.2 = (f32[2048,1,128]{0,2,1:T(8,128)S(1)}, f32[2048,1,128]{0,2,1:T(8,128)}, u32[]{:S(2)}) copy-start(f32[2048,1,128]{0,2,1:T(8,128)} %fusion.226) | copy-start | bytes 3145732 | tf_op jit(solution)/shard_map/while
  558.1 5.0 copy-start.7
  577.0 3.1 copy-start.8
  585.8 52.4 %copy-start.14 = (f32[2,2048,1,128]{3,2,0,1:T(1,128)S(1)}, f32[2,2048,1,128]{3,2,0,1:T(1,128)}, u32[]{:S(2)}) copy-start(f32[2,2048,1,128]{3,2,0,1:T(1,128)} %get-tuple-element.268) | copy-start | bytes 6291460
  689.4 96.8 %all-to-all-start.5 = ((bf16[2,2048,4,128]{3,2,0,1:T(4,128)(2,1)}), bf16[2,2048,4,128]{3,2,0,1:T(4,128)(2,1)}, u32[]{:S(2)}, u32[]{:S(2)}) async-start(bf16[2,2048,4,128]{3,2,0,1:T(4,128)(2,1)} %get-tuple-element.267), calls=%async_computation.5 | async-start | bytes 8388608 | tf_op jit(solution)/shard_map/all_to_all | solution.py:107
  (15 other events, 33.5 us)
where the time goes:
time: 801 us; the launch traced here: 792 us
  waiting for transfers between devices  376 us (47%)
  matrix products  149 us (19%)
  blocking collectives  109 us (14%)
  local copies, waits for them, and re-layouts  77.2 us (10%)
  other arithmetic  42.7 us (5%)
  starting transfers between devices  29.1 us (4%)
    all_to_all x1, waiting for transfers between devices, body(): lax.all_to_all(query, 'seq', split_axis=2, concat_axis=1, tiled=True)  86.7 us
    all_to_all x1, waiting for transfers between devices, body(): lax.all_to_all(scaled, 'seq', split_axis=2, concat_axis=1, tiled=True)  86.7 us
    all_to_all x1, waiting for transfers between devices, body(): lax.all_to_all(query_heads, 'seq', split_axis=1, concat_axis=2, tiled=True)  83.4 us
    all_to_all x1, waiting for transfers between devices, body(): lax.all_to_all(output, 'seq', split_axis=2, concat_axis=1, tiled=True)  80.9 us
    all_to_all x1, blocking collectives, body(): lax.all_to_all(value_heads, 'seq', split_axis=1, concat_axis=2, tiled=True)  52.4 us
    all_to_all x1, blocking collectives, body(): lax.all_to_all(key_heads, 'seq', split_axis=1, concat_axis=2, tiled=True)  51.2 us
    dot_general x8, matrix products, one_block(): jnp.einsum('srij,isrd->jsd', prob_low, g_block, preferred_element_type=jn...  47.3 us
    dot_general x8, matrix products, one_block(): jnp.einsum('isrd,jsd->srij', g_block, value_pre, preferred_element_type=j...  42.4 us
  transfers between devices with their start and end apart: 6, of which 6 were waited for; matrix products, arithmetic and copies ran while one was open for 5% of the time, Pallas kernels for 0%

commit v1 on v0

--- a/solution.py
+++ b/solution.py
@@ -94,7 +94,10 @@
     key_slots = jnp.repeat(keys, copies, axis=2)
     value_slots = jnp.repeat(values, copies, axis=2)
     q_heads, g_heads, o_heads, k_heads, v_heads = (
-        lax.all_to_all(query, "seq", split_axis=2, concat_axis=1, tiled=True),
+        jnp.concatenate(
+            lax.all_to_all(jnp.stack(jnp.split(query, lax.axis_size("seq"), axis=2)), "seq", 0, 0),
+            axis=1,
+        ),
         lax.all_to_all(scaled, "seq", split_axis=2, concat_axis=1, tiled=True),
         lax.all_to_all(output, "seq", split_axis=2, concat_axis=1, tiled=True),
         lax.all_to_all(key_slots, "seq", split_axis=2, concat_axis=1, tiled=True),

time: 801 us -> 801 us (level)
  waiting for transfers between devices: 376 us -> 362 us
  local copies, waits for them, and re-layouts: 77.2 us -> 89.8 us
    unnamed x18 -> x24, local copies, waits for them, and re-layouts: 16.4 us -> 26.2 us
  transfers between devices with their start and end apart: 6 -> 6, of which waited for: 6 -> 6; matrix products, arithmetic and copies ran while one was open for 5% -> 7% of each run, Pallas kernels for 0% -> 0%
where the time goes in v1:
time: 801 us; the launch traced here: 791 us
  waiting for transfers between devices  362 us (45%)
  matrix products  149 us (19%)
  blocking collectives  109 us (14%)
  local copies, waits for them, and re-layouts  89.8 us (11%)
  other arithmetic  42.8 us (5%)
  starting transfers between devices  29.1 us (4%)
    all_to_all x1, waiting for transfers between devices, body(): lax.all_to_all(scaled, 'seq', split_axis=2, concat_axis=1, tiled=True)  86.8 us
    all_to_all x1, waiting for transfers between devices, body(): lax.all_to_all(query_heads, 'seq', split_axis=1, concat_axis=2, tiled=True)  83.4 us
    all_to_all x1, waiting for transfers between devices, body(): lax.all_to_all(jnp.stack(jnp.split(query, lax.axis_size('seq'), axis=2)),...  79.6 us
    all_to_all x1, waiting for transfers between devices, body(): lax.all_to_all(output, 'seq', split_axis=2, concat_axis=1, tiled=True)  74.7 us
    all_to_all x1, blocking collectives, body(): lax.all_to_all(value_heads, 'seq', split_axis=1, concat_axis=2, tiled=True)  52.4 us
    all_to_all x1, blocking collectives, body(): lax.all_to_all(key_heads, 'seq', split_axis=1, concat_axis=2, tiled=True)  51.2 us
    dot_general x8, matrix products, one_block(): jnp.einsum('srij,isrd->jsd', prob_low, g_block, preferred_element_type=jn...  47.3 us
    dot_general x8, matrix products, one_block(): jnp.einsum('isrd,jsd->srij', g_block, value_pre, preferred_element_type=j...  42.4 us
  transfers between devices with their start and end apart: 6, of which 6 were waited for; matrix products, arithmetic and copies ran while one was open for 7% of the time, Pallas kernels for 0%

profile of v1, /device:TPU:0, one launch (start us, length us, event | category | flops | bytes accessed | tf_op | source)
XLA Modules:
  0.0 791.0 jit_solution(15151187246892380342)
XLA Ops:
  3.0 7.3 all-to-all-start
  10.4 25.7 %all-to-all-done = bf16[2,256,8,128]{3,1,0,2:T(8,128)(2,1)S(1)} async-done(((bf16[2,256,8,128]{3,1,0,2:T(8,128)(2,1)}), bf16[2,256,8,128]{3,1,0,2:T(8,128)(2,1)S(1)}, u32[]{:S(2)}, u32[]{:S(2)}) %all-to-all-start) | async-done | bytes 1048608 | tf_op jit(solution)/shard_map/all_to_all | solution.py:103
  41.5 5.6 psum.7
  48.5 5.9 multiply_convert_fusion
  54.5 12.3 %all-to-all-done.2 = bf16[2,256,8,128]{3,1,0,2:T(8,128)(2,1)S(1)} async-done(((bf16[2,256,8,128]{3,1,0,2:T(8,128)(2,1)}), bf16[2,256,8,128]{3,1,0,2:T(8,128)(2,1)S(1)}, u32[]{:S(2)}, u32[]{:S(2)}) %all-to-all-start.2) | async-done | bytes 1048608 | tf_op jit(solution)/shard_map/all_to_all | solution.py:104
  71.3 5.8 copy.194
  77.1 86.8 %all-to-all-done.3 = bf16[2,256,32,128]{3,1,0,2:T(8,128)(2,1)} async-done(((bf16[2,256,32,128]{3,1,0,2:T(8,128)(2,1)}), bf16[2,256,32,128]{3,1,0,2:T(8,128)(2,1)}, u32[]{:S(2)}, u32[]{:S(2)}) %all-to-all-start.3) | async-done | bytes 4194336 | tf_op jit(solution)/shard_map/all_to_all | solution.py:101
  186.3 74.7 %all-to-all-done.4 = bf16[2,256,32,128]{3,1,0,2:T(8,128)(2,1)} async-done(((bf16[2,256,32,128]{3,1,0,2:T(8,128)(2,1)}), bf16[2,256,32,128]{3,1,0,2:T(8,128)(2,1)}, u32[]{:S(2)}, u32[]{:S(2)}) %all-to-all-start.4) | async-done | bytes 4194336 | tf_op jit(solution)/shard_map/all_to_all | solution.py:102
  272.7 5.7 fusion.155
  278.5 79.6 %all-to-all-done.1 = bf16[8,2,256,4,128]{4,3,2,1,0:T(4,128)(2,1)} async-done(((bf16[8,2,256,4,128]{4,3,2,1,0:T(4,128)(2,1)}), bf16[8,2,256,4,128]{4,3,2,1,0:T(4,128)(2,1)}, u32[]{:S(2)}, u32[]{:S(2)}) %all-to-all-start.1) | async-done | bytes 4194336 | tf_op jit(solution)/shard_map/all_to_all | solution.py:98
  358.1 5.2 copy.189
  363.3 221.5 %while.27 = (s32[]{:T(128)}, bf16[2,2048,4,128]{3,2,0,1:T(4,128)(2,1)}, f32[2,2048,1,128]{3,2,0,1:T(1,128)}, f32[2,2048,1,128]{3,2,0,1:T(1,128)}, bf16[2,2048,1,...) while((s32[]{:T(128)}, ...), condition=%wide.region_12.13_spmd, body=%wide.region_3.12_spmd.sunk | while | flops 13606184960 | bytes 444718720 | solution.py:107
  398.4 6.2 fusion.222
  404.7 5.7 fusion.215
  428.2 11.9 %fusion.223 = f32[1,2048,1,128]{1,3,2,0:T(8,128)} fusion(f32[2048,1,128]{0,2,1:T(8,128)} %fusion.222, f32[2048,512,4]{1,0,2:T(8,128)} %copy-done, f32[4,512]{1,0:T(4,128)S(1)} %log_add_fusion.11, pred[512,2048]{0,1:T(8,128)(4,1)S(1)} %copy-done.3, bf16[2,2048,4,128]{3,1,2,0:T(8,128)(2,1)} %get-tuple-element.461, s32[]{:T(128)S(6)} %copy.275, ...), kind=kOutput, calls=%fused_computation.58.clone.1 | convolution fusion | flops 1090781184 | bytes 20455432 | tf_op jit(solution)/shard_map/while/body/eval_jaxpr/srij,isrd->jsd/dot_general | solution.py:39
  440.1 9.0 %fusion.218 = bf16[4,512,2048]{1,2,0:T(8,128)(2,1)S(1)} fusion(f32[2048,512,4]{1,0,2:T(8,128)} %copy-done, f32[4,512]{1,0:T(4,128)S(1)} %get-tuple-element.420, f32[4,512]{1,0:T(4,128)S(1)} %log_add_fusion.11, pred[512,2048]{0,1:T(8,128)(4,1)S(1)} %copy-done.3, bf16[2,2048,1,128]{3,1,2,0:T(8,128)(2,1)S(1)} %copy-done.15, s32[]{:T(128)S(6)} %copy.275, ...), kind=kOutput, calls=%fused_computation.16.clone.1 | convolution fusion | flops 1098907648 | bytes 27280896 | tf_op jit(solution)/shard_map/while/body/eval_jaxpr/isrd,jsd->srij/dot_general | solution.py:42
  506.7 6.0 fusion.222
  512.6 5.7 fusion.215
  536.2 11.9 %fusion.223 = f32[1,2048,1,128]{1,3,2,0:T(8,128)} fusion(f32[2048,1,128]{0,2,1:T(8,128)} %fusion.222, f32[2048,512,4]{1,0,2:T(8,128)} %copy-done, f32[4,512]{1,0:T(4,128)S(1)} %log_add_fusion.11, pred[512,2048]{0,1:T(8,128)(4,1)S(1)} %copy-done.3, bf16[2,2048,4,128]{3,1,2,0:T(8,128)(2,1)} %get-tuple-element.461, s32[]{:T(128)S(6)} %copy.275, ...), kind=kOutput, calls=%fused_computation.58.clone.1 | convolution fusion | flops 1090781184 | bytes 20455432 | tf_op jit(solution)/shard_map/while/body/eval_jaxpr/srij,isrd->jsd/dot_general | solution.py:39
  548.1 9.0 %fusion.218 = bf16[4,512,2048]{1,2,0:T(8,128)(2,1)S(1)} fusion(f32[2048,512,4]{1,0,2:T(8,128)} %copy-done, f32[4,512]{1,0:T(4,128)S(1)} %get-tuple-element.420, f32[4,512]{1,0:T(4,128)S(1)} %log_add_fusion.11, pred[512,2048]{0,1:T(8,128)(4,1)S(1)} %copy-done.3, bf16[2,2048,1,128]{3,1,2,0:T(8,128)(2,1)S(1)} %copy-done.15, s32[]{:T(128)S(6)} %copy.275, ...), kind=kOutput, calls=%fused_computation.16.clone.1 | convolution fusion | flops 1098907648 | bytes 27280896 | tf_op jit(solution)/shard_map/while/body/eval_jaxpr/isrd,jsd->srij/dot_general | solution.py:42
  584.8 52.4 %all_to_all.116 = f32[2,2048,1,128]{3,2,0,1:T(1,128)} all-to-all(f32[2,2048,1,128]{3,2,0,1:T(1,128)} %get-tuple-element.269), channel_id=1, replica_groups=mesh['dp'=4,'seq'=8] {'seq'}, dimensions={1} | all-to-all | bytes 4194304 | tf_op jit(solution)/shard_map/all_to_all | solution.py:113
  637.2 51.2 %all_to_all.117 = f32[2,2048,1,128]{3,2,0,1:T(1,128)S(1)} all-to-all(f32[2,2048,1,128]{3,2,0,1:T(1,128)S(1)} %copy-done.14), channel_id=1, replica_groups=mesh['dp'=4,'seq'=8] {'seq'}, dimensions={1} | all-to-all | bytes 4194304 | tf_op jit(solution)/shard_map/all_to_all | solution.py:112
  701.8 83.4 %all-to-all-done.5 = bf16[2,2048,4,128]{3,2,0,1:T(4,128)(2,1)} async-done(((bf16[2,2048,4,128]{3,2,0,1:T(4,128)(2,1)}), bf16[2,2048,4,128]{3,2,0,1:T(4,128)(2,1)}, u32[]{:S(2)}, u32[]{:S(2)}) %all-to-all-start.5) | async-done | bytes 4194336 | tf_op jit(solution)/shard_map/all_to_all | solution.py:110
  785.3 5.6 copy.199
  (181 shorter events, 209.7 us)
Async XLA Ops:
  0.6 9.7 %copy-start.16 = (bf16[2,256,4,128]{3,2,1,0:T(4,128)(2,1)S(1)}, bf16[2,256,4,128]{3,2,1,0:T(4,128)(2,1)}, u32[]{:S(2)}) copy-start(bf16[2,256,4,128]{3,2,1,0:T(4,128)(2,1)} %param.32) | copy-start | bytes 1572868
  1.8 39.0 %copy-start.17 = (s32[2]{0:T(128)S(1)}, s32[2]{0:T(128)}, u32[]{:S(2)}) copy-start(s32[2]{0:T(128)} %param.35) | copy-start | bytes 28
  1.8 46.6 %copy-start.18 = (f32[2]{0:T(128)S(1)}, f32[2]{0:T(128)}, u32[]{:S(2)}) copy-start(f32[2]{0:T(128)} %constant.334.clone) | copy-start | bytes 28
  3.0 33.0 %all-to-all-start = ((bf16[2,256,8,128]{3,1,0,2:T(8,128)(2,1)}), bf16[2,256,8,128]{3,1,0,2:T(8,128)(2,1)S(1)}, u32[]{:S(2)}, u32[]{:S(2)}) async-start(bf16[2,256,8,128]{3,1,0,2:T(8,128)(2,1)} %bitcast.103), calls=%async_computation | async-start | bytes 2097152 | tf_op jit(solution)/shard_map/all_to_all | solution.py:103
  37.3 29.5 %all-to-all-start.2 = ((bf16[2,256,8,128]{3,1,0,2:T(8,128)(2,1)}), bf16[2,256,8,128]{3,1,0,2:T(8,128)(2,1)S(1)}, u32[]{:S(2)}, u32[]{:S(2)}) async-start(bf16[2,256,8,128]{3,1,0,2:T(8,128)(2,1)} %bitcast.642), calls=%async_computation.2 | async-start | bytes 2097152 | tf_op jit(solution)/shard_map/all_to_all | solution.py:104
  66.8 10.3 %copy-start.11 = (bf16[2,256,8,128]{3,1,0,2:T(8,128)(2,1)}, bf16[2,256,8,128]{3,1,0,2:T(8,128)(2,1)S(1)}, u32[]{:S(2)}) copy-start(bf16[2,256,8,128]{3,1,0,2:T(8,128)(2,1)S(1)} %all-to-all-done.2) | copy-start | bytes 3145732
  66.8 97.1 %all-to-all-start.3 = ((bf16[2,256,32,128]{3,1,0,2:T(8,128)(2,1)}), bf16[2,256,32,128]{3,1,0,2:T(8,128)(2,1)}, u32[]{:S(2)}, u32[]{:S(2)}) async-start(bf16[2,256,32,128]{3,1,0,2:T(8,128)(2,1)} %multiply_convert_fusion), calls=%async_computation.3 | async-start | bytes 8388608 | tf_op jit(solution)/shard_map/all_to_all | solution.py:101
  163.9 97.1 %all-to-all-start.4 = ((bf16[2,256,32,128]{3,1,0,2:T(8,128)(2,1)}), bf16[2,256,32,128]{3,1,0,2:T(8,128)(2,1)}, u32[]{:S(2)}, u32[]{:S(2)}) async-start(bf16[2,256,32,128]{3,1,0,2:T(8,128)(2,1)} %copy.194), calls=%async_computation.4 | async-start | bytes 8388608 | tf_op jit(solution)/shard_map/all_to_all | solution.py:102
  261.0 97.1 %all-to-all-start.1 = ((bf16[8,2,256,4,128]{4,3,2,1,0:T(4,128)(2,1)}), bf16[8,2,256,4,128]{4,3,2,1,0:T(4,128)(2,1)}, u32[]{:S(2)}, u32[]{:S(2)}) async-start(bf16[8,2,256,4,128]{4,3,2,1,0:T(4,128)(2,1)} %bitcast_dynamic-update-slice_fusion), calls=%async_computation.1 | async-start | bytes 8388608 | tf_op jit(solution)/shard_map/all_to_all | solution.py:98
  363.3 30.1 %copy-start.6 = (bf16[2,2048,1,128]{3,1,2,0:T(8,128)(2,1)}, bf16[2,2048,1,128]{3,1,2,0:T(8,128)(2,1)S(1)}, u32[]{:S(2)}) copy-start(bf16[2,2048,1,128]{3,1,2,0:T(8,128)(2,1)S(1)} %get-tuple-element.458) | copy-start | bytes 3145732 | tf_op jit(solution)/shard_map/while
  364.5 34.0 %copy-start.9 = (pred[512,1536]{0,1:T(8,128)(4,1)}, pred[512,1536]{0,1:T(8,128)(4,1)S(1)}, u32[]{:S(2)}) copy-start(pred[512,1536]{0,1:T(8,128)(4,1)S(1)} %iota_compare_fusion.10) | copy-start | bytes 2359300 | tf_op jit(solution)/shard_map/while
  422.5 5.7 copy-start
  428.2 11.9 %copy-start.15 = (bf16[2,2048,1,128]{3,1,2,0:T(8,128)(2,1)S(1)}, bf16[2,2048,1,128]{3,1,2,0:T(8,128)(2,1)}, u32[]{:S(2)}) copy-start(bf16[2,2048,1,128]{3,1,2,0:T(8,128)(2,1)} %get-tuple-element.460) | copy-start | bytes 3145732 | tf_op jit(solution)/shard_map/while
  440.1 9.0 %copy-start.2 = (f32[2048,1,128]{0,2,1:T(8,128)S(1)}, f32[2048,1,128]{0,2,1:T(8,128)}, u32[]{:S(2)}) copy-start(f32[2048,1,128]{0,2,1:T(8,128)} %fusion.226) | copy-start | bytes 3145732 | tf_op jit(solution)/shard_map/while
  449.1 5.0 copy-start.7
  471.3 30.3 %copy-start.6 = (bf16[2,2048,1,128]{3,1,2,0:T(8,128)(2,1)}, bf16[2,2048,1,128]{3,1,2,0:T(8,128)(2,1)S(1)}, u32[]{:S(2)}) copy-start(bf16[2,2048,1,128]{3,1,2,0:T(8,128)(2,1)S(1)} %get-tuple-element.458) | copy-start | bytes 3145732 | tf_op jit(solution)/shard_map/while
  472.5 34.2 %copy-start.9 = (pred[512,1536]{0,1:T(8,128)(4,1)}, pred[512,1536]{0,1:T(8,128)(4,1)S(1)}, u32[]{:S(2)}) copy-start(pred[512,1536]{0,1:T(8,128)(4,1)S(1)} %iota_compare_fusion.10) | copy-start | bytes 2359300 | tf_op jit(solution)/shard_map/while
  530.5 5.7 copy-start
  536.2 11.9 %copy-start.15 = (bf16[2,2048,1,128]{3,1,2,0:T(8,128)(2,1)S(1)}, bf16[2,2048,1,128]{3,1,2,0:T(8,128)(2,1)}, u32[]{:S(2)}) copy-start(bf16[2,2048,1,128]{3,1,2,0:T(8,128)(2,1)} %get-tuple-element.460) | copy-start | bytes 3145732 | tf_op jit(solution)/shard_map/while
  548.1 9.0 %copy-start.2 = (f32[2048,1,128]{0,2,1:T(8,128)S(1)}, f32[2048,1,128]{0,2,1:T(8,128)}, u32[]{:S(2)}) copy-start(f32[2048,1,128]{0,2,1:T(8,128)} %fusion.226) | copy-start | bytes 3145732 | tf_op jit(solution)/shard_map/while
  557.1 5.0 copy-start.7
  576.0 3.1 copy-start.8
  584.8 52.4 %copy-start.14 = (f32[2,2048,1,128]{3,2,0,1:T(1,128)S(1)}, f32[2,2048,1,128]{3,2,0,1:T(1,128)}, u32[]{:S(2)}) copy-start(f32[2,2048,1,128]{3,2,0,1:T(1,128)} %get-tuple-element.268) | copy-start | bytes 6291460
  688.4 96.8 %all-to-all-start.5 = ((bf16[2,2048,4,128]{3,2,0,1:T(4,128)(2,1)}), bf16[2,2048,4,128]{3,2,0,1:T(4,128)(2,1)}, u32[]{:S(2)}, u32[]{:S(2)}) async-start(bf16[2,2048,4,128]{3,2,0,1:T(4,128)(2,1)} %get-tuple-element.267), calls=%async_computation.5 | async-start | bytes 8388608 | tf_op jit(solution)/shard_map/all_to_all | solution.py:110
  (15 other events, 33.5 us)
